TPU v7x, 32 devices: a whole 2x2x4 slice. The times are simulated.
32 devices in a mesh: seq: 8 (over z, x), fsdp: 4 (over y, core).
Axes of the slice: x: 2, y: 2, z: 4, core: 2. Of those that a mesh axis runs over, the one named last changes fastest.
Arguments:
- tokens: bfloat16 [4, 2048, 1536], P('fsdp', 'seq'), may hold values from -6 to 6
- lengths: int32 [4], P('fsdp'), may hold values from 512 to 2048, as said below
- norm_gain: bfloat16 [1536], P('fsdp'), may hold values from 0.099609375 to 1.8984375
- in_weight: bfloat16 [1536, 6448], P('fsdp'), may hold values from -0.15625 to 0.15625
- conv_weight: bfloat16 [4, 3328], P(None, 'fsdp'), may hold values from -3 to 3
- conv_bias: bfloat16 [3328], P('fsdp'), may hold values from -0.5 to 0.5
- dt_bias: bfloat16 [48], P('fsdp'), may hold values from -4.5 to -3.5
- decay_log: bfloat16 [48], P('fsdp'), may hold values from -9 to 0
- skip_gain: bfloat16 [48], P('fsdp'), may hold values from 0.5 to 1.5
- gated_gain: bfloat16 [3072], P('fsdp'), may hold values from 0.099609375 to 1.8984375
- out_weight: bfloat16 [3072, 1536], P('fsdp'), may hold values from -0.109375 to 0.109375
- cotangent: bfloat16 [4, 2048, 1536], P('fsdp', 'seq'), may hold values from -6 to 6
Outputs:
- mixed: bfloat16 [4, 2048, 1536], P('fsdp', 'seq')
- input_grad: float32 [4, 2048, 1536], P('fsdp', 'seq')
- norm_gain_grad: float32 [1536], P('fsdp')
- in_weight_grad: float32 [1536, 6448], P('fsdp')
- conv_weight_grad: float32 [4, 3328], P(None, 'fsdp')
- conv_bias_grad: float32 [3328], P('fsdp')
- dt_bias_grad: float32 [48], P('fsdp')
- decay_log_grad: float32 [48], P('fsdp')
- skip_gain_grad: float32 [48], P('fsdp')
- gated_gain_grad: float32 [3072], P('fsdp')
- out_weight_grad: float32 [3072, 1536], P('fsdp')
Inputs may be any that keep to these rules, and one draw needn't show every extreme that they name: `lengths`: each slot's valid positions come first; some slot has all 2048 valid.
All inputs are finite; a program needn't handle non-finite values.
Results may differ from a plain program's by a relative error of at most 0.012.
The roundings to bfloat16 on the way count: a program that leaves them out, or rounds other values in their place, can miss the bound.
Values may be sent and summed in bfloat16 or wider, within the bound.
No kernel may reach another device: no remote copies, remote signals or barrier semaphores. Data moves between devices by JAX's collectives and lax.ppermute only.
A program may use at most 256 MiB of HBM per device.

v0:
```python
import jax
import jax.numpy as jnp
from jax import lax
from jax.sharding import PartitionSpec as P

epsilon = 1e-05
triple = lax.Precision.HIGH


def from_behind(value, axis, by):
    count = lax.axis_size(axis)
    pairs = [(i, i + by) for i in range(count) if 0 <= i + by < count]
    return lax.ppermute(value, axis, pairs)


def carried_in(value, axis, combine, identity, reverse):
    count, position = (lax.axis_size(axis), lax.axis_index(axis))
    everything = jax.tree.map(lambda part: lax.all_gather(part, axis), value)
    start = jax.tree.map(
        lambda part, zero: jnp.broadcast_to(jnp.asarray(zero, part.dtype), part.shape),
        value,
        identity,
    )

    def lap(k, before):
        at = count - 1 - k if reverse else k
        reached = at > position if reverse else at < position
        new = combine(before, jax.tree.map(lambda part: part[at], everything))
        return jax.tree.map(lambda a, b: jnp.where(reached, a, b), new, before)

    return lax.fori_loop(0, count, lap, start)


def rms_scale(inputs, gain):
    inv_rms = lax.rsqrt(jnp.mean(inputs * inputs, axis=-1, keepdims=True) + epsilon)
    return inputs * inv_rms * gain


def convolve(extended, conv_w, conv_b):
    taps = conv_w.shape[0]
    count = extended.shape[1] - taps + 1
    summed = conv_b + jnp.zeros(extended[:, :count].shape, jnp.float32)
    for offset in range(taps):
        summed = summed + extended[:, offset : offset + count] * conv_w[offset]
    return jax.nn.silu(summed)


def local_scan(values, b_rows, c_rows, step_raw, dt_b, decay_l):
    step_size = jax.nn.softplus(step_raw + dt_b)
    log_decay = jnp.cumsum(-step_size * jnp.exp(decay_l), axis=1)
    count = values.shape[1]
    places = jnp.arange(count)
    lower = (places[:, None] >= places[None, :])[None, :, :, None]
    gaps = log_decay[:, :, None, :] - log_decay[:, None, :, :]
    weights = jnp.where(lower, jnp.exp(jnp.where(lower, gaps, 0.0)), 0.0)
    intersection = jnp.einsum("stn,sun->stu", c_rows, b_rows, precision=triple)
    mixing = weights * intersection[..., None] * step_size[:, None, :, :]
    local_out = jnp.einsum("stuh,suhp->sthp", mixing, values, precision=triple)
    to_end = jnp.exp(log_decay[:, -1:, :] - log_decay) * step_size
    local_state = jnp.einsum("sqh,sqhp,sqn->shpn", to_end, values, b_rows, precision=triple)
    return (local_out, local_state, jnp.exp(log_decay[:, -1, :]), jnp.exp(log_decay))


def finish(local_out, c_rows, decay_in, state_in, values, skip_g, gate_part, gated_g):
    carried_out = decay_in[..., None] * jnp.einsum(
        "sqn,shpn->sqhp", c_rows, state_in, precision=triple
    )
    mixed_heads = local_out + carried_out + skip_g[:, None] * values
    flat = mixed_heads.reshape(gate_part.shape)
    return rms_scale(flat * jax.nn.silu(gate_part), gated_g)


def chain(earlier, later):
    return (earlier[0] * later[0], later[0][..., None, None] * earlier[1] + later[1])


def per_device(
    tokens,
    lengths,
    norm_gain,
    in_weight,
    conv_weight,
    conv_bias,
    dt_bias,
    decay_log,
    skip_gain,
    gated_gain,
    out_weight,
    cotangent,
):
    gathered = (
        lax.all_gather(norm_gain, "fsdp", axis=0, tiled=True),
        lax.all_gather(in_weight, "fsdp", axis=0, tiled=True),
        lax.all_gather(conv_weight, "fsdp", axis=1, tiled=True),
        lax.all_gather(conv_bias, "fsdp", axis=0, tiled=True),
        lax.all_gather(dt_bias, "fsdp", axis=0, tiled=True),
        lax.all_gather(decay_log, "fsdp", axis=0, tiled=True),
        lax.all_gather(skip_gain, "fsdp", axis=0, tiled=True),
        lax.all_gather(gated_gain, "fsdp", axis=0, tiled=True),
        lax.all_gather(out_weight, "fsdp", axis=0, tiled=True),
    )
    full_in = gathered[1]
    full_out = gathered[8]
    norm_f, conv_wf, conv_bf, dtb_f, decay_f, skip_f, ggain_f = [
        gathered[index].astype(jnp.float32) for index in (0, 2, 3, 4, 5, 6, 7)
    ]
    slots, seg, width = tokens.shape
    inner = full_out.shape[0]
    heads = dtb_f.shape[0]
    head_size = inner // heads
    conv_width = conv_wf.shape[1]
    state_width = (conv_width - inner) // 2
    taps = conv_wf.shape[0]
    places = lax.axis_index("seq") * seg + jnp.arange(seg)
    valid = (places[None, :] < lengths[:, None]).astype(jnp.float32)
    inputs = tokens.astype(jnp.float32)
    normed_f, pull_norm = jax.vjp(rms_scale, inputs, norm_f)
    normed = normed_f.astype(jnp.bfloat16)
    projected = jnp.einsum(
        "sqd,dp->sqp", normed, full_in, preferred_element_type=jnp.float32
    ).astype(jnp.bfloat16)
    gate_part = projected[..., :inner].astype(jnp.float32)
    conv_in = projected[..., inner : inner + conv_width]
    step_raw = projected[..., inner + conv_width :].astype(jnp.float32)
    previous = from_behind(conv_in[:, seg - (taps - 1) :], "seq", 1)
    extended = jnp.concatenate([previous, conv_in], axis=1).astype(jnp.float32)
    activated_f, pull_conv = jax.vjp(convolve, extended, conv_wf, conv_bf)
    activated = lax.optimization_barrier(activated_f.astype(jnp.bfloat16)).astype(jnp.float32)
    values = activated[..., :inner].reshape(slots, seg, heads, head_size)
    b_rows = activated[..., inner : inner + state_width]
    c_rows = activated[..., inner + state_width :]
    scanned, pull_local = jax.vjp(local_scan, values, b_rows, c_rows, step_raw, dtb_f, decay_f)
    local_out, local_state, whole_decay, decay_in = scanned
    identity = (
        jnp.ones((slots, heads), jnp.float32),
        jnp.zeros((slots, heads, head_size, state_width), jnp.float32),
    )
    state_in = carried_in((whole_decay, local_state), "seq", chain, identity, False)[1]
    gated_f, pull_finish = jax.vjp(
        finish, local_out, c_rows, decay_in, state_in, values, skip_f, gate_part, ggain_f
    )
    gated_out = gated_f.astype(jnp.bfloat16)
    branch = jnp.einsum("sqi,id->sqd", gated_out, full_out, preferred_element_type=jnp.float32)
    mixed = (valid[..., None] * (inputs + branch)).astype(jnp.bfloat16)
    back_in, back_out = (
        lax.all_gather(in_weight, "fsdp", axis=0, tiled=True),
        lax.all_gather(out_weight, "fsdp", axis=0, tiled=True),
    )
    upstream = valid[..., None] * cotangent.astype(jnp.float32)
    back_branch = upstream.astype(jnp.bfloat16)
    grad_out_w = jnp.einsum(
        "sqi,sqd->id", gated_out, back_branch, preferred_element_type=jnp.float32
    )
    back_gated = jnp.einsum(
        "sqd,id->sqi", back_branch, back_out, preferred_element_type=jnp.float32
    )
    d_local, d_crows_one, d_decay_in, d_state_local, d_values_one, d_skip, d_gate, d_ggain = (
        pull_finish(back_gated)
    )
    state_after = carried_in((whole_decay, d_state_local), "seq", chain, identity, True)[1]
    d_whole = jnp.sum(state_after * state_in, axis=(2, 3))
    d_values_two, d_brows, d_crows_two, d_step, d_dtb, d_decay = pull_local(
        (d_local, state_after, d_whole, d_decay_in)
    )
    d_active = jnp.concatenate(
        [
            (d_values_one + d_values_two).reshape(slots, seg, inner),
            d_brows,
            d_crows_one + d_crows_two,
        ],
        axis=-1,
    )
    d_extended, d_conv_w, d_conv_b = pull_conv(d_active)
    returned = from_behind(d_extended[:, : taps - 1].astype(jnp.bfloat16), "seq", -1).astype(
        jnp.float32
    )
    d_conv_in = d_extended[:, taps - 1 :] + jnp.pad(returned, ((0, 0), (seg - taps + 1, 0), (0, 0)))
    back_projected = jnp.concatenate([d_gate, d_conv_in, d_step], axis=-1).astype(jnp.bfloat16)
    grad_in_w = jnp.einsum(
        "sqd,sqp->dp", normed, back_projected, preferred_element_type=jnp.float32
    )
    back_normed = jnp.einsum(
        "sqp,dp->sqd", back_projected, back_in, preferred_element_type=jnp.float32
    )
    d_inputs, d_norm = pull_norm(back_normed)
    input_grad = upstream + d_inputs
    shares = (
        lax.psum_scatter(d_norm, "fsdp", scatter_dimension=0, tiled=True),
        lax.psum_scatter(grad_in_w, "fsdp", scatter_dimension=0, tiled=True),
        lax.psum_scatter(d_conv_w, "fsdp", scatter_dimension=1, tiled=True),
        lax.psum_scatter(d_conv_b, "fsdp", scatter_dimension=0, tiled=True),
        lax.psum_scatter(d_dtb, "fsdp", scatter_dimension=0, tiled=True),
        lax.psum_scatter(d_decay, "fsdp", scatter_dimension=0, tiled=True),
        lax.psum_scatter(d_skip, "fsdp", scatter_dimension=0, tiled=True),
        lax.psum_scatter(d_ggain, "fsdp", scatter_dimension=0, tiled=True),
        lax.psum_scatter(grad_out_w, "fsdp", scatter_dimension=0, tiled=True),
    )
    totals = lax.psum(
        (
            shares[0],
            shares[1],
            shares[2],
            shares[3],
            shares[4],
            shares[5],
            shares[6],
            shares[7],
            shares[8],
        ),
        "seq",
    )
    return (
        mixed,
        input_grad,
        totals[0],
        totals[1],
        totals[2],
        totals[3],
        totals[4],
        totals[5],
        totals[6],
        totals[7],
        totals[8],
    )


def solution(mesh):
    placed = (
        P("fsdp", "seq", None),
        P("fsdp"),
        P("fsdp"),
        P("fsdp", None),
        P(None, "fsdp"),
        P("fsdp"),
        P("fsdp"),
        P("fsdp"),
        P("fsdp"),
        P("fsdp"),
        P("fsdp", None),
        P("fsdp", "seq", None),
    )
    return jax.shard_map(
        per_device,
        mesh=mesh,
        in_specs=placed,
        out_specs=(
            P("fsdp", "seq", None),
            P("fsdp", "seq", None),
            P("fsdp"),
            P("fsdp", None),
            P(None, "fsdp"),
            P("fsdp"),
            P("fsdp"),
            P("fsdp"),
            P("fsdp"),
            P("fsdp"),
            P("fsdp", None),
        ),
        check_vma=False,
    )
```

profile of v0, /device:TPU:0, one launch (start us, length us, event | category | flops | bytes accessed | tf_op | source)
XLA Modules:
  0.0 1545.1 jit_solution(13398759697782761256)
XLA Ops:
  8.1 6.2 all-gather.3
  22.8 7.5 all-reduce.24
  32.0 105.5 %all-gather.10.cloned.1.call-done = bf16[1536,6448]{0,1:T(8,128)(2,1)} async-done(((bf16[384,6448]{0,1:T(8,128)(2,1)}), bf16[1536,6448]{0,1:T(8,128)(2,1)}) %all-gather.10.cloned.1.call-update) | async-done | bytes 19808272 | tf_op jit(solution)/shard_map/all_gather | solution.py:93
  137.4 9.9 fusion.6
  193.9 19.2 %all_gather.53 = f32[8,1,48]{2,1,0:T(1,128)} all-gather(f32[1,1,48]{2,1,0:T(1,128)} %get-tuple-element.423), channel_id=1, replica_groups=mesh['seq'=8,'fsdp'=4] {'seq'}, dimensions={0}, use_global_device_ids=true | all-gather | bytes 1728 | tf_op jit(solution)/shard_map/all_gather | solution.py:18
  218.5 131.1 %all-gather.14.cloned.1.call-done = f32[384,64,128]{2,1,0:T(8,128)} async-done(((f32[48,64,128]{2,1,0:T(8,128)}), f32[384,64,128]{2,1,0:T(8,128)}) %all-gather.14.cloned.1.call-update) | async-done | bytes 12582928 | tf_op jit(solution)/shard_map/all_gather | solution.py:18
  349.6 36.0 %while.30 = (s32[]{:T(128)}, f32[1,48,64,128]{3,2,1,0:T(8,128)}, s32[]{:T(128)}, f32[8,1,48]{2,1,0:T(1,128)}, f32[8,1,48,64,128]{4,3,2,1,0:T(8,128)}, /*index=5*/s32[]{:T(128)}, s32[]{:T(128)}) while((s32[]{:T(128)}, f32[1,48,64,128]{3,2,1,0:T(8,128)}, s32[]{:T(128)}, f32[8,1,48]{2,1,0:T(1,128)}, f32[8,1,48,64,128]{4,3,2,1,0:T(8,128)}, ...), condition=%wide.region_4.5_spmd.clone, body=%wide.region_3.4_spmd.clone.sunk | while | flops 1572868 | bytes 4719281 | solution.py:31
  388.6 9.6 fusion.34
  413.7 10.0 fusion.35
  423.7 5.9 multiply_reduce_fusion.5
  440.9 12.7 fusion.76
  457.7 14.9 fusion.8
  491.7 125.8 %all-gather.16.cloned.1.call-done = f32[384,64,128]{2,1,0:T(8,128)} async-done(((f32[48,64,128]{2,1,0:T(8,128)}), f32[384,64,128]{2,1,0:T(8,128)}) %all-gather.16.cloned.1.call-update) | async-done | bytes 12582928 | tf_op jit(solution)/shard_map/all_gather | solution.py:18
  617.5 38.9 %while.31 = (s32[]{:T(128)}, f32[1,48,64,128]{3,2,1,0:T(8,128)}, s32[]{:T(128)}, f32[8,1,48]{2,1,0:T(1,128)}, f32[8,1,48,64,128]{4,3,2,1,0:T(8,128)}, /*index=5*/s32[]{:T(128)}, s32[]{:T(128)}, s32[]{:T(128)}, s32[]{:T(128)}) while((s32[]{:T(128)}, f32[1,48,64,128]{3,2,1,0:T(8,128)}, s32[]{:T(128)}, f32[8,1,48]{2,1,0:T(1,128)}, ...), condition=%wide.region_8.9_spmd.clone, body=%wide.region_7.8_spmd.clone.sunk | while | flops 1572872 | bytes 4719343 | solution.py:31
  676.4 11.2 fusion.33
  712.6 18.4 %fusion.61 = f32[1536,6448]{0,1:T(8,128)} fusion(bf16[256,48]{1,0:T(8,128)(2,1)} %bitcast.336, bf16[256,3328]{1,0:T(8,128)(2,1)} %fusion.42, bf16[256,3072]{1,0:T(8,128)(2,1)} %get-tuple-element.412, bf16[1,256,1536]{2,1,0:T(8,128)(2,1)} %param.16, f32[1536]{0:T(1024)S(1)} %reshape.620, f32[256]{0:T(256)S(1)} %fusion.111), kind=kOutput, calls=%fused_computation.114 | convolution fusion | flops 5082390528 | bytes 43711488 | tf_op jit(solution)/shard_map/sqd,sqp->dp/dot_general | solution.py:179
  733.8 23.9 %reduce-scatter.8.cloned.1.call-done = f32[768,1536]{1,0:T(8,128)} async-done(((f32[3072,1536]{1,0:T(8,128)}), f32[768,1536]{1,0:T(8,128)}) %reduce-scatter.8.cloned.1.call-update) | async-done | bytes 4718608 | tf_op jit(solution)/shard_map/reduce_scatter | solution.py:196
  757.6 279.1 %reduce-scatter.6.cloned.1.call-done = f32[384,6448]{0,1:T(8,128)} async-done(((f32[1536,6448]{0,1:T(8,128)}), f32[384,6448]{0,1:T(8,128)}) %reduce-scatter.6.cloned.1.call-update) | async-done | bytes 9904144 | tf_op jit(solution)/shard_map/reduce_scatter | solution.py:189
  1040.0 7.5 fusion.39
  1047.6 10.0 fusion.44
  1057.6 12.3 all-reduce.23
  1073.3 39.6 %all-reduce.21 = (f32[384]{0:T(512)}, f32[4,832]{1,0:T(4,128)}, f32[832]{0:T(1024)}, f32[12]{0:T(128)}, f32[12]{0:T(128)}, /*index=5*/f32[12]{0:T(128)}, f32[768]{0:T(1024)}) all-reduce(f32[384]{0:T(512)S(1)} %dynamic-slice.5, f32[4,832]{1,0:T(4,128)S(1)} %copy.211, ...), channel_id=1, replica_groups=mesh['seq'=8,'fsdp'=4] {'seq'}, use_global_device_ids=true, to_apply=%region_21.22 | all-reduce | flops 5348 | bytes 42784 | tf_op jit(solution)/shard_map/psum | solution.py:198
  1112.9 414.5 %all-reduce.27.cloned.1.call-done = (f32[384,6448]{0,1:T(8,128)}, f32[768,1536]{1,0:T(8,128)}) async-done(((f32[384,6448]{0,1:T(8,128)}, f32[768,1536]{1,0:T(8,128)}), (f32[384,6448]{0,1:T(8,128)}, f32[768,1536]{1,0:T(8,128)})) %all-reduce.27.cloned.1.call-update) | async-done | bytes 14622736 | tf_op jit(solution)/shard_map/psum | solution.py:198
  1527.4 8.5 copy.231
  (294 shorter events, 241.7 us)
Async XLA Ops:
  7.2 12.7 copy-start.52
  7.2 14.6 copy-start.59
  7.2 14.8 copy-start.60
  7.2 15.1 copy-start.61
  7.2 15.3 copy-start.53
  7.3 24.4 %copy-start.11 = (bf16[1,256,1536]{2,1,0:T(8,128)(2,1)S(1)}, bf16[1,256,1536]{2,1,0:T(8,128)(2,1)}, u32[]{:S(2)}) copy-start(bf16[1,256,1536]{2,1,0:T(8,128)(2,1)} %param.16) | copy-start | bytes 2359300
  7.3 130.2 %all-gather.10.cloned.1.call-start = ((), (), s32[]{:S(2)}) async-start(), calls=%async_computation.3 | async-start | bytes 24760320 | tf_op jit(solution)/shard_map/all_gather | solution.py:93
  8.0 341.6 %all-gather.14.cloned.1.call-start = ((), (), s32[]{:S(2)}) async-start(), calls=%async_computation.7 | async-start | bytes 14155776 | tf_op jit(solution)/shard_map/all_gather | solution.py:18
  30.3 117.0 %copy-start.62 = (bf16[48]{0:T(256)(128)(2,1)}, bf16[48]{0:T(256)(128)(2,1)S(1)}, u32[]{:S(2)}) copy-start(bf16[48]{0:T(256)(128)(2,1)S(1)} %get-tuple-element.398) | copy-start | bytes 292
  30.9 125.8 %copy-start.40 = (f32[48]{0:T(128)}, f32[48]{0:T(128)S(1)}, u32[]{:S(2)}) copy-start(f32[48]{0:T(128)S(1)} %convert_element_type.95) | copy-start | bytes 580
  31.9 115.4 %copy-start.44 = (f32[256]{0:T(256)}, f32[256]{0:T(256)S(1)}, u32[]{:S(2)}) copy-start(f32[256]{0:T(256)S(1)} %fusion.46) | copy-start | bytes 3076
  31.9 115.4 %copy-start.55 = (f32[48]{0:T(128)}, f32[48]{0:T(128)S(1)}, u32[]{:S(2)}) copy-start(f32[48]{0:T(128)S(1)} %convert_exponential_fusion) | copy-start | bytes 580
  147.3 12.2 copy-start.10
  151.5 8.1 collective-permute-start
  174.5 239.2 %all-gather.12.cloned.1.call-start = ((), (), s32[]{:S(2)}) async-start(), calls=%async_computation.4 | async-start | bytes 11796480 | tf_op jit(solution)/shard_map/all_gather | solution.py:100
  175.2 442.3 %all-gather.16.cloned.1.call-start = ((), (), s32[]{:S(2)}) async-start(), calls=%async_computation.8 | async-start | bytes 14155776 | tf_op jit(solution)/shard_map/all_gather | solution.py:18
  440.9 316.7 %reduce-scatter.8.cloned.1.call-start = ((), (), s32[]{:S(2)}) async-start(), calls=%async_computation.6 | async-start | bytes 23592960 | tf_op jit(solution)/shard_map/reduce_scatter | solution.py:196
  453.7 583.1 %reduce-scatter.6.cloned.1.call-start = ((), (), s32[]{:S(2)}) async-start(), calls=%async_computation.5 | async-start | bytes 49520640 | tf_op jit(solution)/shard_map/reduce_scatter | solution.py:189
  704.4 6.0 collective-permute-start.1
  731.1 341.0 %reduce-scatter.10.cloned.1.call-start = ((), (), s32[]{:S(2)}) async-start(), calls=%async_computation.9 | async-start | bytes 2129920
  733.7 793.7 %all-reduce.27.cloned.1.call-start = ((), (), s32[]{:S(2)}) async-start(), calls=%async_computation.10 | async-start | bytes 29245440 | tf_op jit(solution)/shard_map/psum | solution.py:198
  1047.6 22.8 %copy-start.45 = (f32[256]{0:T(256)S(1)}, f32[256]{0:T(256)}, u32[]{:S(2)}) copy-start(f32[256]{0:T(256)} %copy-done.44) | copy-start | bytes 3076
  1047.6 22.8 %copy-start.13 = (bf16[1,256,1536]{2,1,0:T(8,128)(2,1)S(1)}, bf16[1,256,1536]{2,1,0:T(8,128)(2,1)}, u32[]{:S(2)}) copy-start(bf16[1,256,1536]{2,1,0:T(8,128)(2,1)} %param.16) | copy-start | bytes 2359300
  1047.6 22.8 %copy-start.20 = (bf16[1,256,1536]{2,1,0:T(8,128)(2,1)S(1)}, bf16[1,256,1536]{2,1,0:T(8,128)(2,1)}, u32[]{:S(2)}) copy-start(bf16[1,256,1536]{2,1,0:T(8,128)(2,1)} %param.27) | copy-start | bytes 2359300
  (51 other events, 259.4 us)
Sparse Core Ops, SparseCore 0:
  9.7 127.6 all-gather.9
  174.6 174.9 all-gather.13
  351.2 62.4 all-gather.11
  441.0 176.4 all-gather.15
  619.9 137.6 reduce-scatter.7
  760.3 276.4 reduce-scatter.5
  1039.9 29.6 reduce-scatter.9
  1074.5 452.8 all-reduce.26
where the time goes:
time: 1550 us
  waiting for transfers between devices  1090 us (70%)
  matrix products  135 us (9%)
  other arithmetic  113 us (7%)
  blocking collectives  95.4 us (6%)
  local copies, waits for them, and re-layouts  88.4 us (6%)
  between operations  20.1 us (1%)
    psum x1, waiting for transfers between devices, per_device(): lax.psum((shares[0], shares[1], shares[2], shares[3], shares[4], shares[5...  415 us
    reduce_scatter x1, waiting for transfers between devices, per_device(): lax.psum_scatter(grad_in_w, 'fsdp', scatter_dimension=0, tiled=True)  279 us
    all_gather x2, waiting for transfers between devices, carried_in(): everything = jax.tree.map(lambda part: lax.all_gather(part, axis), value)  257 us
    all_gather x1, waiting for transfers between devices, per_device(): lax.all_gather(in_weight, 'fsdp', axis=0, tiled=True)  105 us
    select_n x16, other arithmetic, lap(): return jax.tree.map(lambda a, b: jnp.where(reached, a, b), new, before)  56.7 us
    psum x1, blocking collectives, per_device(): lax.psum((shares[0], shares[1], shares[2], shares[3], shares[4], shares[5...  39.6 us
    dot_general x3, matrix products, local_scan(): local_out = jnp.einsum('stuh,suhp->sthp', mixing, values, precision=triple)  35.7 us
  transfers between devices with their start and end apart: 10, of which 8 were waited for; matrix products, arithmetic and copies ran while one was open for 17% of the time, Pallas kernels for 0%

commit v1 on v0

--- a/solution.py
+++ b/solution.py
@@ -5,6 +5,18 @@
 
 epsilon = 1e-05
 triple = lax.Precision.HIGH
+
+
+def collect(x, axis, dim):
+    ways, here = (lax.axis_size(axis), lax.axis_index(axis))
+    grown, reach = (x, 1)
+    while reach < ways:
+        theirs = lax.ppermute(grown, axis, [(d, d ^ reach) for d in range(ways)])
+        mine_first = jnp.concatenate([grown, theirs], axis=dim)
+        theirs_first = jnp.concatenate([theirs, grown], axis=dim)
+        grown = jnp.where(here & reach == 0, mine_first, theirs_first)
+        reach = 2 * reach
+    return grown
 
 
 def from_behind(value, axis, by):
@@ -90,7 +102,7 @@
 ):
     gathered = (
         lax.all_gather(norm_gain, "fsdp", axis=0, tiled=True),
-        lax.all_gather(in_weight, "fsdp", axis=0, tiled=True),
+        collect(in_weight, "fsdp", 0),
         lax.all_gather(conv_weight, "fsdp", axis=1, tiled=True),
         lax.all_gather(conv_bias, "fsdp", axis=0, tiled=True),
         lax.all_gather(dt_bias, "fsdp", axis=0, tiled=True),

time: 1550 us -> 1820 us (1.17)
  blocking collectives: 95.4 us -> 302 us
  waiting for transfers between devices: 1090 us -> 1110 us
    all_gather x1, blocking collectives: 6.22 us -> 214 us  [per_device(): lax.all_gather(conv_weight, 'fsdp', axis=1, tiled=True)]
  transfers between devices with their start and end apart: 10 -> 12, of which waited for: 8 -> 10; matrix products, arithmetic and copies ran while one was open for 17% -> 15% of each run, Pallas kernels for 0% -> 0%
where the time goes in v1:
time: 1820 us; the launch traced here: 1810 us
  waiting for transfers between devices  1110 us (61%)
  blocking collectives  302 us (17%)
  matrix products  146 us (8%)
  other arithmetic  126 us (7%)
  local copies, waits for them, and re-layouts  87.8 us (5%)
  between operations  20.2 us (1%)
    psum x1, waiting for transfers between devices, per_device(): lax.psum((shares[0], shares[1], shares[2], shares[3], shares[4], shares[5...  418 us
    reduce_scatter x1, waiting for transfers between devices, per_device(): lax.psum_scatter(grad_in_w, 'fsdp', scatter_dimension=0, tiled=True)  279 us
    all_gather x2, waiting for transfers between devices, carried_in(): everything = jax.tree.map(lambda part: lax.all_gather(part, axis), value)  249 us
    all_gather x1, blocking collectives, per_device(): lax.all_gather(conv_weight, 'fsdp', axis=1, tiled=True)  214 us
    all_gather x1, waiting for transfers between devices, per_device(): lax.all_gather(in_weight, 'fsdp', axis=0, tiled=True)  116 us
    select_n x16, other arithmetic, lap(): return jax.tree.map(lambda a, b: jnp.where(reached, a, b), new, before)  56.9 us
    psum x1, blocking collectives, per_device(): lax.psum((shares[0], shares[1], shares[2], shares[3], shares[4], shares[5...  39.2 us
  transfers between devices with their start and end apart: 12, of which 10 were waited for; matrix products, arithmetic and copies ran while one was open for 15% of the time, Pallas kernels for 0%

profile of v1, /device:TPU:0, one launch (start us, length us, event | category | flops | bytes accessed | tf_op | source)
XLA Modules:
  0.0 1806.6 jit_solution(8370006020926846153)
XLA Ops:
  7.8 8.2 collective-permute-done
  16.0 13.1 maximum_select_fusion.2
  32.0 214.5 %all-gather.3 = bf16[4,832,4]{1,2,0:T(4,128)(2,1)S(1)} all-gather(bf16[1,832,4]{1,2,0:T(4,128)(2,1)S(1)} %bitcast.342), channel_id=1, replica_groups=mesh['seq'=8,'fsdp'=4] {'fsdp'}, dimensions={0}, use_global_device_ids=true | all-gather | bytes 33280 | tf_op jit(solution)/shard_map/all_gather | solution.py:106
  263.9 18.2 %fusion.14 = bf16[1,256,6448]{2,1,0:T(8,128)(2,1)S(1)} fusion(bf16[768,6448]{0,1:T(8,128)(2,1)} %collective-permute-done.1, bf16[768,6448]{0,1:T(8,128)(2,1)} %maximum_select_fusion.2, pred[]{:T(512)S(6)} %eq.14, bf16[1,256,1536]{2,1,0:T(8,128)(2,1)} %param.16, f32[1536]{0:T(1024)S(1)} %reshape.620, f32[256]{0:T(256)S(1)} %fusion.119), kind=kOutput, calls=%fused_computation.26 | convolution fusion | flops 5163274240 | bytes 23903232 | tf_op jit(solution)/shard_map/sqd,dp->sqp/dot_general | solution.py:131
  328.8 19.5 %all_gather.51 = f32[8,1,48]{2,1,0:T(1,128)} all-gather(f32[1,1,48]{2,1,0:T(1,128)} %get-tuple-element.423), channel_id=1, replica_groups=mesh['seq'=8,'fsdp'=4] {'seq'}, dimensions={0}, use_global_device_ids=true | all-gather | bytes 1728 | tf_op jit(solution)/shard_map/all_gather | solution.py:30
  353.6 131.1 %all-gather.14.cloned.1.call-done = f32[384,64,128]{2,1,0:T(8,128)} async-done(((f32[48,64,128]{2,1,0:T(8,128)}), f32[384,64,128]{2,1,0:T(8,128)}) %all-gather.14.cloned.1.call-update) | async-done | bytes 12582928 | tf_op jit(solution)/shard_map/all_gather | solution.py:30
  484.8 36.0 %while.30 = (s32[]{:T(128)}, f32[1,48,64,128]{3,2,1,0:T(8,128)}, s32[]{:T(128)}, f32[8,1,48]{2,1,0:T(1,128)}, f32[8,1,48,64,128]{4,3,2,1,0:T(8,128)}, /*index=5*/s32[]{:T(128)}, s32[]{:T(128)}) while((s32[]{:T(128)}, f32[1,48,64,128]{3,2,1,0:T(8,128)}, s32[]{:T(128)}, f32[8,1,48]{2,1,0:T(1,128)}, f32[8,1,48,64,128]{4,3,2,1,0:T(8,128)}, ...), condition=%wide.region_4.5_spmd.clone, body=%wide.region_3.4_spmd.clone.sunk | while | flops 1572868 | bytes 4719281 | solution.py:43
  523.8 9.6 fusion.42
  548.8 10.1 fusion.43
  576.2 12.7 fusion.84
  588.9 8.7 reduce-scatter.6.cloned.1.call-start
  601.3 14.9 fusion.16
  635.3 117.4 %all-gather.16.cloned.1.call-done = f32[384,64,128]{2,1,0:T(8,128)} async-done(((f32[48,64,128]{2,1,0:T(8,128)}), f32[384,64,128]{2,1,0:T(8,128)}) %all-gather.16.cloned.1.call-update) | async-done | bytes 12582928 | tf_op jit(solution)/shard_map/all_gather | solution.py:30
  752.7 39.0 %while.31 = (s32[]{:T(128)}, f32[1,48,64,128]{3,2,1,0:T(8,128)}, s32[]{:T(128)}, f32[8,1,48]{2,1,0:T(1,128)}, f32[8,1,48,64,128]{4,3,2,1,0:T(8,128)}, /*index=5*/s32[]{:T(128)}, s32[]{:T(128)}, s32[]{:T(128)}, s32[]{:T(128)}) while((s32[]{:T(128)}, f32[1,48,64,128]{3,2,1,0:T(8,128)}, s32[]{:T(128)}, f32[8,1,48]{2,1,0:T(1,128)}, ...), condition=%wide.region_8.9_spmd.clone, body=%wide.region_7.8_spmd.clone.sunk | while | flops 1572872 | bytes 4719343 | solution.py:43
  811.8 11.0 fusion.41
  847.8 18.5 %fusion.69 = f32[1536,6448]{0,1:T(8,128)} fusion(bf16[256,48]{1,0:T(8,128)(2,1)} %bitcast.335, bf16[256,3328]{1,0:T(8,128)(2,1)} %fusion.50, bf16[256,3072]{1,0:T(8,128)(2,1)} %get-tuple-element.412, bf16[1,256,1536]{2,1,0:T(8,128)(2,1)} %param.16, f32[1536]{0:T(1024)S(1)} %reshape.620, f32[256]{0:T(256)S(1)} %fusion.119), kind=kOutput, calls=%fused_computation.123 | convolution fusion | flops 5082390528 | bytes 43711488 | tf_op jit(solution)/shard_map/sqd,sqp->dp/dot_general | solution.py:191
  869.0 23.8 %reduce-scatter.8.cloned.1.call-done = f32[768,1536]{1,0:T(8,128)} async-done(((f32[3072,1536]{1,0:T(8,128)}), f32[768,1536]{1,0:T(8,128)}) %reduce-scatter.8.cloned.1.call-update) | async-done | bytes 4718608 | tf_op jit(solution)/shard_map/reduce_scatter | solution.py:208
  892.8 279.1 %reduce-scatter.6.cloned.1.call-done = f32[384,6448]{0,1:T(8,128)} async-done(((f32[1536,6448]{0,1:T(8,128)}), f32[384,6448]{0,1:T(8,128)}) %reduce-scatter.6.cloned.1.call-update) | async-done | bytes 9904144 | tf_op jit(solution)/shard_map/reduce_scatter | solution.py:201
  1182.6 115.7 %all-gather.12.cloned.1.call-done = bf16[1536,6448]{0,1:T(8,128)(2,1)} async-done(((bf16[384,6448]{0,1:T(8,128)(2,1)}), bf16[1536,6448]{0,1:T(8,128)(2,1)}) %all-gather.12.cloned.1.call-update) | async-done | bytes 19808272 | tf_op jit(solution)/shard_map/all_gather | solution.py:158
  1298.3 13.3 fusion.52
  1311.6 11.3 all-reduce.23
  1331.9 39.2 %all-reduce.21 = (f32[384]{0:T(512)}, f32[4,832]{1,0:T(4,128)}, f32[832]{0:T(1024)}, f32[12]{0:T(128)}, f32[12]{0:T(128)}, /*index=5*/f32[12]{0:T(128)}, f32[768]{0:T(1024)}) all-reduce(f32[384]{0:T(512)S(1)} %dynamic-slice.5, f32[4,832]{1,0:T(4,128)S(1)} %copy.211, ...), channel_id=1, replica_groups=mesh['seq'=8,'fsdp'=4] {'seq'}, use_global_device_ids=true, to_apply=%region_21.22 | all-reduce | flops 5348 | bytes 42784 | tf_op jit(solution)/shard_map/psum | solution.py:210
  1371.1 417.6 %all-reduce.27.cloned.1.call-done = (f32[384,6448]{0,1:T(8,128)}, f32[768,1536]{1,0:T(8,128)}) async-done(((f32[384,6448]{0,1:T(8,128)}, f32[768,1536]{1,0:T(8,128)}), (f32[384,6448]{0,1:T(8,128)}, f32[768,1536]{1,0:T(8,128)})) %all-reduce.27.cloned.1.call-update) | async-done | bytes 14622736 | tf_op jit(solution)/shard_map/psum | solution.py:210
  1788.7 8.5 copy.231
  (293 shorter events, 270.6 us)
Async XLA Ops:
  7.2 477.6 %all-gather.14.cloned.1.call-start = ((), (), s32[]{:S(2)}) async-start(), calls=%async_computation.7 | async-start | bytes 14155776 | tf_op jit(solution)/shard_map/all_gather | solution.py:30
  7.2 8.7 collective-permute-start
  7.7 238.9 %copy-start.54 = (bf16[384]{0:T(512)(128)(2,1)S(1)}, bf16[384]{0:T(512)(128)(2,1)}, u32[]{:S(2)}) copy-start(bf16[384]{0:T(512)(128)(2,1)} %param.18) | copy-start | bytes 2308
  7.7 244.1 %copy-start.49 = (u32[32]{0:T(128)S(1)}, u32[32]{0:T(128)}, u32[]{:S(2)}) copy-start(u32[32]{0:T(128)} %constant.145) | copy-start | bytes 388
  7.7 246.0 %copy-start.56 = (bf16[12]{0:T(256)(128)(2,1)S(1)}, bf16[12]{0:T(256)(128)(2,1)}, u32[]{:S(2)}) copy-start(bf16[12]{0:T(256)(128)(2,1)} %param.23) | copy-start | bytes 76
  7.8 246.3 %copy-start.57 = (bf16[12]{0:T(256)(128)(2,1)S(1)}, bf16[12]{0:T(256)(128)(2,1)}, u32[]{:S(2)}) copy-start(bf16[12]{0:T(256)(128)(2,1)} %param.22) | copy-start | bytes 76
  7.8 246.5 %copy-start.58 = (bf16[12]{0:T(256)(128)(2,1)S(1)}, bf16[12]{0:T(256)(128)(2,1)}, u32[]{:S(2)}) copy-start(bf16[12]{0:T(256)(128)(2,1)} %param.24) | copy-start | bytes 76
  7.8 246.7 %copy-start.50 = (bf16[832]{0:T(1024)(128)(2,1)S(1)}, bf16[832]{0:T(1024)(128)(2,1)}, u32[]{:S(2)}) copy-start(bf16[832]{0:T(1024)(128)(2,1)} %param.21) | copy-start | bytes 4996
  7.8 255.9 %copy-start.11 = (bf16[1,256,1536]{2,1,0:T(8,128)(2,1)S(1)}, bf16[1,256,1536]{2,1,0:T(8,128)(2,1)}, u32[]{:S(2)}) copy-start(bf16[1,256,1536]{2,1,0:T(8,128)(2,1)} %param.16) | copy-start | bytes 2359300
  29.1 234.8 %collective-permute-start.1 = (bf16[768,6448]{0,1:T(8,128)(2,1)}, bf16[768,6448]{0,1:T(8,128)(2,1)}, u32[]{:S(2)}, u32[]{:S(2)}) collective-permute-start(bf16[768,6448]{0,1:T(8,128)(2,1)} %maximum_select_fusion.2), channel_id=1, source_target_pairs={{0,2},{1,3},{2,0},{3,1},{4,6},{5,7},{6,4},{7,5},{8,10},{9,11},{10,... | collective-permute-start | bytes 29712392 | tf_op jit(solution)/shard_map/ppermute | solution.py:14
  286.3 8.1 collective-permute-start.2
  309.4 239.4 %all-gather.10.cloned.1.call-start = ((), (), s32[]{:S(2)}) async-start(), calls=%async_computation.3 | async-start | bytes 11796480 | tf_op jit(solution)/shard_map/all_gather | solution.py:112
  310.1 442.6 %all-gather.16.cloned.1.call-start = ((), (), s32[]{:S(2)}) async-start(), calls=%async_computation.8 | async-start | bytes 14155776 | tf_op jit(solution)/shard_map/all_gather | solution.py:30
  576.1 316.7 %reduce-scatter.8.cloned.1.call-start = ((), (), s32[]{:S(2)}) async-start(), calls=%async_computation.6 | async-start | bytes 23592960 | tf_op jit(solution)/shard_map/reduce_scatter | solution.py:208
  588.9 583.0 %reduce-scatter.6.cloned.1.call-start = ((), (), s32[]{:S(2)}) async-start(), calls=%async_computation.5 | async-start | bytes 49520640 | tf_op jit(solution)/shard_map/reduce_scatter | solution.py:201
  839.5 6.0 collective-permute-start.3
  866.4 431.9 %all-gather.12.cloned.1.call-start = ((), (), s32[]{:S(2)}) async-start(), calls=%async_computation.4 | async-start | bytes 24760320 | tf_op jit(solution)/shard_map/all_gather | solution.py:158
  867.0 463.7 %reduce-scatter.10.cloned.1.call-start = ((), (), s32[]{:S(2)}) async-start(), calls=%async_computation.9 | async-start | bytes 2129920
  869.0 919.7 %all-reduce.27.cloned.1.call-start = ((), (), s32[]{:S(2)}) async-start(), calls=%async_computation.10 | async-start | bytes 29245440 | tf_op jit(solution)/shard_map/psum | solution.py:210
  1182.6 129.0 %copy-start.29 = (f32[3328]{0:T(1024)S(1)}, f32[3328]{0:T(1024)}, u32[]{:S(2)}) copy-start(f32[3328]{0:T(1024)} %get-tuple-element.355) | copy-start | bytes 39940
  1182.6 129.0 %copy-start.39 = (f32[3072]{0:T(1024)S(1)}, f32[3072]{0:T(1024)}, u32[]{:S(2)}) copy-start(f32[3072]{0:T(1024)} %get-tuple-element.353) | copy-start | bytes 36868
  1182.6 140.7 %copy-start.42 = (f32[256]{0:T(256)S(1)}, f32[256]{0:T(256)}, u32[]{:S(2)}) copy-start(f32[256]{0:T(256)} %copy-done.41) | copy-start | bytes 3076
  1182.6 140.7 %copy-start.12 = (bf16[1,256,1536]{2,1,0:T(8,128)(2,1)S(1)}, bf16[1,256,1536]{2,1,0:T(8,128)(2,1)}, u32[]{:S(2)}) copy-start(bf16[1,256,1536]{2,1,0:T(8,128)(2,1)} %param.16) | copy-start | bytes 2359300
  1182.6 140.7 %copy-start.17 = (bf16[1,256,1536]{2,1,0:T(8,128)(2,1)S(1)}, bf16[1,256,1536]{2,1,0:T(8,128)(2,1)}, u32[]{:S(2)}) copy-start(bf16[1,256,1536]{2,1,0:T(8,128)(2,1)} %param.27) | copy-start | bytes 2359300
  (50 other events, 564.6 us)
Sparse Core Ops, SparseCore 0:
  309.5 175.2 all-gather.13
  486.3 62.4 all-gather.9
  576.2 176.4 all-gather.15
  755.1 137.6 reduce-scatter.7
  895.5 276.4 reduce-scatter.5
  1173.4 124.8 all-gather.11
  1301.4 29.2 reduce-scatter.9
  1335.6 453.0 all-reduce.26
